TPU v7x, 32 devices: a whole 2x2x4 slice. The times are simulated.
32 devices in a mesh: dp: 8 (over y, x, core), expert: 4 (over z).
Axes of the slice: x: 2, y: 2, z: 4, core: 2. Of those that a mesh axis runs over, the one named last changes fastest.
Arguments:
- tokens: bfloat16 [4096, 2048], P(('dp', 'expert')), may hold values from -6 to 6
- w_qkv: bfloat16 [3, 2048, 2048], P(None, 'dp', 'expert'), may hold values from -0.125 to 0.125
- w_out: bfloat16 [2048, 2048], P('expert', 'dp'), may hold values from -0.5 to 0.5
- attention_norm_gain: bfloat16 [2048], P('dp'), may hold values from 0.5 to 1.5
- gain_ffn: bfloat16 [2048], P('dp'), may hold values from 0.5 to 1.5
- w_router: bfloat16 [2048, 4], P('dp'), may hold values from -0.09375 to 0.09375
- w_gate_up: bfloat16 [4, 2048, 11264], P('expert', 'dp'), may hold values from -0.125 to 0.125
- w_down: bfloat16 [4, 5632, 2048], P('expert', 'dp'), may hold values from -0.15625 to 0.15625
- lengths: int32 [8], P('dp'), may hold values from 128 to 512, as said below
- routes: int32 [4096, 2], P(('dp', 'expert')), may hold values from 0 to 3, all different within a row
- order: int32 [4096], P(('dp', 'expert')), may hold values from 0 to 127, as said below
- cotangent: bfloat16 [4096, 2048], P(('dp', 'expert')), may hold values from -6 to 6
Outputs:
- output: bfloat16 [4096, 2048], P(('dp', 'expert'))
- grad_tokens: bfloat16 [4096, 2048], P(('dp', 'expert'))
- grad_qkv: float32 [3, 2048, 2048], P(None, 'dp', 'expert')
- grad_out: float32 [2048, 2048], P('expert', 'dp')
- grad_gain_attn: float32 [2048], P('dp')
- grad_gain_ffn: float32 [2048], P('dp')
- grad_router: float32 [2048, 4], P('dp')
- grad_gate_up: float32 [4, 2048, 11264], P('expert', 'dp')
- grad_down: float32 [4, 5632, 2048], P('expert', 'dp')
Inputs may be any that keep to these rules, and one draw needn't show every extreme that they name: `lengths`: one sequence of every draw has exactly 512 live tokens. `routes`: each token slot names 2 different experts, and every expert is named somewhere. `order`: each aligned block of 128 entries holds every number of 0 to 127 once.
All inputs are finite; a program needn't handle non-finite values.
Results may differ from a plain program's by a relative error of at most 0.023.
Values may be sent and summed in bfloat16 or wider, within the bound.
A program may use at most 384 MiB of HBM per device.

v0:
```python
import jax
import jax.numpy as jnp
from jax import lax
from jax.sharding import PartitionSpec as P

HEAD_DIM = 128
FF = 5632
NORM_EPSILON = 1e-05
NEGATIVE = -1e30
THETA = 10000.0
HIGH = lax.Precision.HIGHEST


def rotary_tables(length_total, head_size):
    position = jnp.arange(length_total, dtype=jnp.float32)
    frequency = THETA ** (-(jnp.arange(head_size // 2, dtype=jnp.float32) * 2.0 / head_size))
    angles = position[:, None] * frequency[None, :]
    return (jnp.cos(angles)[:, None, :], jnp.sin(angles)[:, None, :])


def rotate(values, cosine, sine):
    half_size = values.shape[-1] // 2
    first = values[..., :half_size]
    second = values[..., half_size:]
    return jnp.concatenate(
        [first * cosine - second * sine, second * cosine + first * sine], axis=-1
    )


def rotate_back(grad_rows, cosine, sine):
    half_size = grad_rows.shape[-1] // 2
    first = grad_rows[..., :half_size]
    second = grad_rows[..., half_size:]
    return jnp.concatenate(
        [first * cosine + second * sine, second * cosine - first * sine], axis=-1
    )


def slot_table(routes, order, valid, capacity):
    row_count = routes.shape[0]
    top_count = routes.shape[1]
    pair_rank = order[:, None] + row_count * jnp.arange(top_count, dtype=jnp.int32)[None, :]
    flat_rank = pair_rank.reshape(-1)
    flat_expert = routes.reshape(-1)
    flat_valid = jnp.broadcast_to(valid[:, None], routes.shape).reshape(-1)
    earlier = (
        (flat_rank[None, :] < flat_rank[:, None])
        & (flat_expert[None, :] == flat_expert[:, None])
        & flat_valid[None, :]
    )
    slot_index = jnp.sum(earlier.astype(jnp.int32), axis=1).reshape(row_count, top_count)
    kept_pair = valid[:, None] & (slot_index < capacity)
    target = routes * capacity + jnp.minimum(slot_index, capacity - 1)
    return (target, kept_pair)


def masked_scores(query, key_rows, allowed):
    scale = query.shape[-1] ** (-0.5)
    raw = jnp.einsum("qhd,khd->hqk", query, key_rows, preferred_element_type=jnp.float32) * scale
    return jnp.where(allowed[None], raw, NEGATIVE)


def contract_first(left, right):
    return lax.dot_general(
        left, right, (((0,), (0,)), ((), ())), preferred_element_type=jnp.float32
    )


def contract_last(left, right):
    return lax.dot_general(
        left, right, (((1,), (1,)), ((), ())), preferred_element_type=jnp.float32
    )


def normalize(rows):
    inverse = lax.rsqrt(jnp.mean(rows * rows, axis=-1, keepdims=True) + NORM_EPSILON)
    return (rows * inverse, inverse)


def exchange_experts(blocks):
    return lax.all_to_all(blocks, "expert", split_axis=0, concat_axis=0, tiled=True)


def by_hidden(w_gate_up):
    parts = lax.axis_size("dp")
    rows = w_gate_up.shape[1]
    ff_part = w_gate_up.shape[2] // 2 // parts
    pieces = w_gate_up[0].reshape(rows, 2, parts, ff_part).transpose(2, 0, 1, 3)
    pieces = pieces.reshape(parts, rows, 2 * ff_part)
    got = lax.all_to_all(pieces, "dp", split_axis=0, concat_axis=0, tiled=True)
    return got.reshape(parts * rows, 2 * ff_part)


def by_rows(grad):
    parts = lax.axis_size("dp")
    rows = grad.shape[0] // parts
    ff_part = grad.shape[1] // 2
    pieces = grad.astype(jnp.bfloat16).reshape(parts, rows, 2 * ff_part)
    got = lax.all_to_all(pieces, "dp", split_axis=0, concat_axis=0, tiled=True)
    got = got.reshape(parts, rows, 2, ff_part).transpose(1, 2, 0, 3)
    return got.reshape(1, rows, 2 * parts * ff_part).astype(jnp.float32)


def expert_step(gate_up_w, down_w, rows, d_rows_out):
    ff = down_w.shape[0]
    gate_up = jnp.dot(rows, gate_up_w, preferred_element_type=jnp.float32)
    gate = gate_up[:, :ff]
    upward = gate_up[:, ff:]
    sigmoid = jax.nn.sigmoid(gate)
    activated = (gate * sigmoid * upward).astype(jnp.bfloat16)
    out = jnp.dot(activated, down_w, preferred_element_type=jnp.float32).astype(jnp.bfloat16)
    d_activated = contract_last(d_rows_out, down_w)
    grad_down = contract_first(activated, d_rows_out)
    d_gate = d_activated * upward * sigmoid * (1.0 + gate * (1.0 - sigmoid))
    d_up = d_activated * gate * sigmoid
    d_gate_up = jnp.concatenate([d_gate, d_up], axis=1).astype(jnp.bfloat16)
    d_rows = contract_last(d_gate_up, gate_up_w).astype(jnp.bfloat16)
    grad_gate_up = contract_first(rows, d_gate_up)
    return (out, d_rows, grad_gate_up, grad_down)


def experts_split_hidden(w_gate_up, w_down, rows, d_rows_out):
    gate_up_w = by_hidden(w_gate_up)
    all_rows = lax.all_gather(rows, "dp", axis=0, tiled=True)
    all_d_out = lax.all_gather(d_rows_out, "dp", axis=0, tiled=True)
    out, d_rows, grad_gate_up, grad_down = expert_step(gate_up_w, w_down[0], all_rows, all_d_out)
    out = lax.psum_scatter(out, "dp", scatter_dimension=0, tiled=True)
    d_rows = lax.psum_scatter(d_rows, "dp", scatter_dimension=0, tiled=True)
    return (out, d_rows, by_rows(grad_gate_up), grad_down[None])


def experts_gather_weights(w_gate_up, w_down, rows, d_rows_out):
    gate_up_w = lax.all_gather(w_gate_up, "dp", axis=1, tiled=True)[0]
    down_w = lax.all_gather(w_down, "dp", axis=1, tiled=True)[0]
    out, d_rows, grad_gate_up, grad_down = expert_step(gate_up_w, down_w, rows, d_rows_out)
    grad_gate_up = lax.psum_scatter(
        grad_gate_up.astype(jnp.bfloat16), "dp", scatter_dimension=0, tiled=True
    )
    grad_down = lax.psum_scatter(
        grad_down.astype(jnp.bfloat16), "dp", scatter_dimension=0, tiled=True
    )
    return (
        out,
        d_rows,
        grad_gate_up.astype(jnp.float32)[None],
        grad_down.astype(jnp.float32)[None],
    )


def on_device(
    tokens,
    w_qkv,
    w_out,
    attention_norm_gain,
    gain_ffn,
    w_router,
    w_gate_up,
    w_down,
    lengths,
    routes,
    order,
    cotangent,
):
    group_size = lax.axis_size("expert")
    dp_size = lax.axis_size("dp")
    tok_dev = tokens.shape[0]
    seq_len = tok_dev * group_size
    width = tokens.shape[1]
    top_count = routes.shape[1]
    capacity = tok_dev * top_count // group_size
    slots = group_size * capacity
    head_size = HEAD_DIM
    local_width = w_qkv.shape[2]
    heads_local = local_width // head_size
    tokens_all = lax.all_gather(tokens, "expert", axis=0, tiled=True)
    small = jnp.concatenate([attention_norm_gain[:, None], gain_ffn[:, None], w_router], axis=1)
    small_full = lax.all_gather(small, "dp", axis=0, tiled=True)
    qkv_full = lax.all_gather(w_qkv, "dp", axis=1, tiled=True)
    out_full = lax.all_gather(w_out, "dp", axis=1, tiled=True)
    first_norm_gain = small_full[:, 0].astype(jnp.float32)
    gain_two = small_full[:, 1].astype(jnp.float32)
    router_full = small_full[:, 2:]
    own_start = lax.axis_index("expert") * tok_dev
    own_position = own_start + jnp.arange(tok_dev, dtype=jnp.int32)
    live_own = own_position < lengths[0]
    live_rows = live_own.astype(jnp.float32)[:, None]
    target, kept_pair = slot_table(routes, order, live_own, capacity)
    slot_ids = jnp.arange(slots, dtype=jnp.int32)
    pair_hits = (slot_ids[:, None, None] == target[None]) & kept_pair[None]
    select = jnp.sum(pair_hits.astype(jnp.float32), axis=2).astype(jnp.bfloat16)
    inputs_float = tokens.astype(jnp.float32)
    input_normalized_hat, first_inverse_rms = normalize(inputs_float)
    hat_all, _ = normalize(tokens_all.astype(jnp.float32))
    whole = (hat_all * first_norm_gain).astype(jnp.bfloat16)
    cosine, sine = rotary_tables(seq_len, head_size)
    projected = jnp.einsum("td,cde->cte", whole, qkv_full, preferred_element_type=jnp.float32)
    query = rotate(projected[0].reshape(seq_len, heads_local, head_size), cosine, sine).astype(
        jnp.bfloat16
    )
    key_rows = rotate(projected[1].reshape(seq_len, heads_local, head_size), cosine, sine).astype(
        jnp.bfloat16
    )
    value = projected[2].astype(jnp.bfloat16).reshape(seq_len, heads_local, head_size)
    position = jnp.arange(seq_len, dtype=jnp.int32)
    live_all = position < lengths[0]
    allowed = (position[None, :] <= position[:, None]) & live_all[None, :]
    scores = masked_scores(query, key_rows, allowed)
    top_score = jnp.max(scores, axis=-1, keepdims=True)
    exponent = jnp.exp(scores - top_score)
    row_total = jnp.sum(exponent, axis=-1, keepdims=True)
    probs = exponent / row_total
    log_total = top_score + jnp.log(row_total)
    probs_low = probs.astype(jnp.bfloat16)
    attended = jnp.einsum("hqk,khd->qhd", probs_low, value, preferred_element_type=jnp.float32)
    attended = attended.reshape(seq_len, local_width).astype(jnp.bfloat16)
    attn_part = jnp.dot(attended, out_full, preferred_element_type=jnp.float32)
    attn_own = lax.psum_scatter(
        attn_part.astype(jnp.bfloat16), "expert", scatter_dimension=0, tiled=True
    ).astype(jnp.float32)
    resid = inputs_float + attn_own
    hhat, inverse_two = normalize(resid)
    hidden_in = (hhat * gain_two).astype(jnp.bfloat16)
    sent = jnp.dot(select, hidden_in, preferred_element_type=jnp.float32).astype(jnp.bfloat16)
    dispatched = exchange_experts(sent.reshape(group_size, capacity, width)).reshape(slots, width)
    logits = jnp.dot(hidden_in, router_full, preferred_element_type=jnp.float32)
    chosen = jnp.take_along_axis(logits, routes, axis=1)
    gates = jax.nn.softmax(chosen, axis=1)
    d_out = live_rows * cotangent.astype(jnp.float32)
    d_back = jnp.zeros((slots, width), jnp.float32)
    for index in range(top_count):
        weighted = (gates[:, index : index + 1] * d_out).astype(jnp.bfloat16)
        d_back = d_back + jnp.dot(
            pair_hits[:, :, index].astype(jnp.bfloat16),
            weighted,
            preferred_element_type=jnp.float32,
        )
    d_back = d_back.astype(jnp.bfloat16)
    d_out_rows = exchange_experts(d_back.reshape(group_size, capacity, width)).reshape(slots, width)
    split_cost = 4 * dp_size * slots * width + 2 * 2 * FF * width // dp_size
    gather_cost = 2 * 3 * FF * width
    experts = experts_split_hidden if split_cost < gather_cost else experts_gather_weights
    expert_out, d_rows, grad_gate_up, grad_down = experts(w_gate_up, w_down, dispatched, d_out_rows)
    d_sent = exchange_experts(d_rows.reshape(group_size, capacity, width)).reshape(slots, width)
    returned = exchange_experts(expert_out.reshape(group_size, capacity, width)).reshape(
        slots, width
    )
    moe = jnp.zeros_like(resid)
    d_gates_list = []
    for index in range(top_count):
        one_hot = pair_hits[:, :, index].astype(jnp.bfloat16)
        picked = contract_first(one_hot, returned)
        d_gates_list.append(jnp.sum(d_out * picked, axis=-1))
        moe = moe + gates[:, index : index + 1] * picked
    output = (live_rows * (resid + moe)).astype(jnp.bfloat16)
    d_gates = jnp.stack(d_gates_list, axis=1)
    d_hidden = contract_first(select, d_sent)
    d_chosen = gates * (d_gates - jnp.sum(gates * d_gates, axis=1, keepdims=True))
    expert_ids = jnp.arange(group_size, dtype=jnp.int32)
    route_hits = (routes[:, :, None] == expert_ids[None, None, :]).astype(jnp.float32)
    d_logits = jnp.sum(route_hits * d_chosen[:, :, None], axis=1)
    router_f = router_full.astype(jnp.float32)
    d_hidden = d_hidden + jnp.dot(
        d_logits, router_f.T, precision=HIGH, preferred_element_type=jnp.float32
    )
    router_part = jnp.dot(
        hidden_in.astype(jnp.float32).T,
        d_logits,
        precision=HIGH,
        preferred_element_type=jnp.float32,
    )
    gain_two_part = jnp.sum(d_hidden * hhat, axis=0)
    scaled_two = d_hidden * gain_two
    d_resid = d_out + inverse_two * (
        scaled_two - hhat * jnp.mean(scaled_two * hhat, axis=-1, keepdims=True)
    )
    d_attn = d_resid.astype(jnp.bfloat16)
    whole_grad = lax.all_gather(d_attn, "expert", axis=0, tiled=True)
    d_attended = contract_last(whole_grad, out_full).astype(jnp.bfloat16)
    out_part = contract_first(attended, whole_grad)
    grad_out = lax.psum_scatter(
        out_part.astype(jnp.bfloat16), "dp", scatter_dimension=1, tiled=True
    ).astype(jnp.float32)
    d_heads = d_attended.reshape(seq_len, heads_local, head_size)
    probs = jnp.exp(masked_scores(query, key_rows, allowed) - log_total)
    probs_low = probs.astype(jnp.bfloat16)
    d_value = jnp.einsum(
        "hqk,qhd->khd", probs_low, d_heads, preferred_element_type=jnp.float32
    ).astype(jnp.bfloat16)
    d_probs = jnp.einsum("qhd,khd->hqk", d_heads, value, preferred_element_type=jnp.float32)
    row_delta = jnp.sum(probs * d_probs, axis=-1, keepdims=True)
    d_scores = (probs * (d_probs - row_delta)).astype(jnp.bfloat16)
    scale = head_size ** (-0.5)
    d_query = (
        jnp.einsum("hqk,khd->qhd", d_scores, key_rows, preferred_element_type=jnp.float32) * scale
    )
    d_key = jnp.einsum("hqk,qhd->khd", d_scores, query, preferred_element_type=jnp.float32) * scale
    d_query_pre = (
        rotate_back(d_query, cosine, sine).reshape(seq_len, local_width).astype(jnp.bfloat16)
    )
    d_key_pre = rotate_back(d_key, cosine, sine).reshape(seq_len, local_width).astype(jnp.bfloat16)
    d_projected = jnp.stack([d_query_pre, d_key_pre, d_value.reshape(seq_len, local_width)])
    d_normed_part = jnp.einsum(
        "cte,cde->td", d_projected, qkv_full, preferred_element_type=jnp.float32
    )
    grad_normalized = lax.psum_scatter(
        d_normed_part.astype(jnp.bfloat16), "expert", scatter_dimension=0, tiled=True
    ).astype(jnp.float32)
    qkv_part = jnp.einsum("td,cte->cde", whole, d_projected, preferred_element_type=jnp.float32)
    grad_qkv = lax.psum_scatter(
        qkv_part.astype(jnp.bfloat16), "dp", scatter_dimension=1, tiled=True
    ).astype(jnp.float32)
    first_gain_part = jnp.sum(d_normed_part * hat_all, axis=0)
    first_scaled_input = grad_normalized * first_norm_gain
    grad_tokens = d_resid + first_inverse_rms * (
        first_scaled_input
        - input_normalized_hat
        * jnp.mean(first_scaled_input * input_normalized_hat, axis=-1, keepdims=True)
    )
    small_part = jnp.concatenate(
        [first_gain_part[None], gain_two_part[None], router_part.T], axis=0
    )
    small_sum = lax.psum(small_part, ("dp", "expert"))
    own_rows = width // dp_size
    small_own = lax.dynamic_slice_in_dim(
        small_sum, lax.axis_index("dp") * own_rows, own_rows, axis=1
    )
    return (
        output,
        grad_tokens.astype(jnp.bfloat16),
        grad_qkv,
        grad_out,
        small_own[0],
        small_own[1],
        small_own[2:].T,
        grad_gate_up,
        grad_down,
    )


def solution(mesh):
    placed = (
        P(("dp", "expert"), None),
        P(None, "dp", "expert"),
        P("expert", "dp"),
        P("dp"),
        P("dp"),
        P("dp", None),
        P("expert", "dp", None),
        P("expert", "dp", None),
        P("dp"),
        P(("dp", "expert"), None),
        P(("dp", "expert")),
        P(("dp", "expert"), None),
    )
    return jax.shard_map(
        on_device,
        mesh=mesh,
        in_specs=placed,
        out_specs=(
            P(("dp", "expert"), None),
            P(("dp", "expert"), None),
            P(None, "dp", "expert"),
            P("expert", "dp"),
            P("dp"),
            P("dp"),
            P("dp", None),
            P("expert", "dp", None),
            P("expert", "dp", None),
        ),
        check_vma=False,
    )
```

profile of v0, /device:TPU:10, one launch (start us, length us, event | category | flops | bytes accessed | tf_op | source)
XLA Modules:
  0.0 981.0 jit_solution(3513390332413267402)
XLA Ops:
  8.0 2.4 copy.213
  13.8 9.1 all_gather.22
  23.8 1.7 fusion.41
  25.5 29.6 %all-gather.7.cloned.1.call-done = bf16[512,2048]{1,0:T(8,128)(2,1)} async-done(((bf16[128,2048]{1,0:T(8,128)(2,1)}), bf16[512,2048]{1,0:T(8,128)(2,1)}) %all-gather.7.cloned.1.call-update) | async-done | bytes 2097168 | tf_op jit(solution)/shard_map/all_gather | solution.py:175
  55.1 2.1 fusion.4
  57.2 47.4 %all-gather.9.cloned.1.call-done = bf16[3,2048,512]{1,2,0:T(8,128)(2,1)} async-done(((bf16[3,256,512]{1,2,0:T(8,128)(2,1)}), bf16[3,2048,512]{1,2,0:T(8,128)(2,1)}) %all-gather.9.cloned.1.call-update) | async-done | bytes 6291472 | tf_op jit(solution)/shard_map/all_gather | solution.py:178
  104.6 6.4 convolution_bitcast_fusion.1
  113.9 2.4 copy.260
  116.2 2.2 fusion.66
  118.5 2.4 copy.262
  120.8 1.3 copy.259
  122.2 2.4 copy.261
  124.5 3.3 subtract_convert_fusion.3
  127.8 1.4 fusion.68
  129.9 1.4 copy-done.2
  131.3 1.7 fusion.21
  133.0 1.7 all-gather.11.cloned.1.call-done
  134.7 4.4 convolution_convert_fusion.4
  141.3 39.6 %reduce-scatter.7.cloned.1.call-done = bf16[128,2048]{1,0:T(8,128)(2,1)} async-done(((bf16[512,2048]{1,0:T(8,128)(2,1)}), bf16[128,2048]{1,0:T(8,128)(2,1)}) %reduce-scatter.7.cloned.1.call-update) | async-done | bytes 524304 | tf_op jit(solution)/shard_map/reduce_scatter | solution.py:217
  180.9 1.3 multiply_reduce_fusion.5
  184.7 30.0 %all_to_all.30 = bf16[4,64,2048]{2,1,0:T(8,128)(2,1)} all-to-all(bf16[4,64,2048]{2,1,0:T(8,128)(2,1)S(1)} %bitcast.127), channel_id=1, replica_groups=mesh['dp'=8,'expert'=4] {'expert'}, dimensions={0} | all-to-all | bytes 2097152 | tf_op jit(solution)/shard_map/all_to_all | solution.py:81
  215.0 8.4 copy.224
  223.4 3.4 copy.225
  226.8 94.9 %all_to_all.31 = bf16[8,256,1408]{1,2,0:T(8,128)(2,1)} all-to-all(bf16[8,256,1408]{1,2,0:T(8,128)(2,1)S(1)} %bitcast.119), channel_id=1, replica_groups=mesh['dp'=8,'expert'=4] {'dp'}, dimensions={0} | all-to-all | bytes 11534336 | tf_op jit(solution)/shard_map/all_to_all | solution.py:90
  321.7 8.2 copy.226
  329.9 18.8 %fusion.69 = f32[2048,1408]{0,1:T(8,128)} fusion(bf16[2048,2048]{1,0:T(8,128)(2,1)} %all-gather.13.cloned.1.call-done, bf16[2048,1408]{1,0:T(8,128)(2,1)} %bitcast.121), kind=kOutput, calls=%fused_computation.161 | convolution fusion | flops 11811160064 | bytes 25690112 | tf_op jit(solution)/shard_map/dot_general | solution.py:106
  348.7 5.2 multiply_convert_fusion.2
  354.0 1.7 copy-done.22
  355.7 9.1 convolution_convert_fusion.1
  364.7 71.4 %reduce-scatter.9.cloned.1.call-done = bf16[256,2048]{1,0:T(8,128)(2,1)} async-done(((bf16[2048,2048]{1,0:T(8,128)(2,1)}), bf16[256,2048]{1,0:T(8,128)(2,1)}) %reduce-scatter.9.cloned.1.call-update) | async-done | bytes 1048592 | tf_op jit(solution)/shard_map/reduce_scatter | solution.py:127
  436.1 5.1 all-to-all-start.2
  443.9 2.4 gather_fusion
  447.1 1.5 copy.220
  449.8 13.9 %all-to-all-done.2 = bf16[4,64,2048]{2,1,0:T(8,128)(2,1)} async-done(((bf16[4,64,2048]{2,1,0:T(8,128)(2,1)}), bf16[4,64,2048]{2,1,0:T(8,128)(2,1)}, u32[]{:S(2)}, u32[]{:S(2)}) %all-to-all-start.2) | async-done | bytes 1048608 | tf_op jit(solution)/shard_map/all_to_all | solution.py:81
  463.7 1.6 fusion.44
  466.3 2.8 multiply_reduce_fusion.4
  471.4 29.9 %all_to_all.32 = bf16[4,64,2048]{2,1,0:T(8,128)(2,1)} all-to-all(bf16[4,64,2048]{2,1,0:T(8,128)(2,1)S(1)} %bitcast.130), channel_id=1, replica_groups=mesh['dp'=8,'expert'=4] {'expert'}, dimensions={0} | all-to-all | bytes 2097152 | tf_op jit(solution)/shard_map/all_to_all | solution.py:81
  501.4 54.0 %all-gather.15.cloned.1.call-done = bf16[2048,2048]{1,0:T(8,128)(2,1)} async-done(((bf16[256,2048]{1,0:T(8,128)(2,1)}), bf16[2048,2048]{1,0:T(8,128)(2,1)}) %all-gather.15.cloned.1.call-update) | async-done | bytes 8388624 | tf_op jit(solution)/shard_map/all_gather | solution.py:125
  555.4 13.1 %multiply_convert_fusion.1 = (bf16[2048,704]{0,1:T(8,128)(2,1)S(1)}, bf16[2048,704]{0,1:T(8,128)(2,1)S(1)}) fusion(f32[2048,1408]{0,1:T(8,128)} %fusion.69, bf16[2048,2048]{1,0:T(8,128)(2,1)} %all-gather.15.cloned.1.call-done, bf16[1,704,2048]{2,1,0:T(8,128)(2,1)S(1)} %copy-done), kind=kOutput, calls=%fused_computation.8 | convolution fusion | flops 5924323328 | bytes 28573696 | tf_op jit(solution)/shard_map/dot_general | solution.py:70
  568.5 1.5 copy-done.62
  570.9 17.7 %convolution_convert_fusion = bf16[2048,2048]{1,0:T(8,128)(2,1)} fusion(bf16[2048,1408]{1,0:T(8,128)(2,1)} %bitcast.122, bf16[2048,704]{0,1:T(8,128)(2,1)S(1)} %get-tuple-element.75, bf16[2048,704]{0,1:T(8,128)(2,1)S(1)} %get-tuple-element.74), kind=kOutput, calls=%fused_computation.2 | convolution fusion | flops 11826888704 | bytes 19922944 | tf_op jit(solution)/shard_map/dot_general | solution.py:70
  588.7 71.3 %reduce-scatter.11.cloned.1.call-done = bf16[256,2048]{1,0:T(8,128)(2,1)} async-done(((bf16[2048,2048]{1,0:T(8,128)(2,1)}), bf16[256,2048]{1,0:T(8,128)(2,1)}) %reduce-scatter.11.cloned.1.call-update) | async-done | bytes 1048592 | tf_op jit(solution)/shard_map/reduce_scatter | solution.py:128
  660.0 5.1 all-to-all-start.4
  665.4 22.2 %all-to-all-done.4 = bf16[4,64,2048]{2,1,0:T(8,128)(2,1)S(1)} async-done(((bf16[4,64,2048]{2,1,0:T(8,128)(2,1)}), bf16[4,64,2048]{2,1,0:T(8,128)(2,1)S(1)}, u32[]{:S(2)}, u32[]{:S(2)}) %all-to-all-start.4) | async-done | bytes 1048608 | tf_op jit(solution)/shard_map/all_to_all | solution.py:81
  690.4 45.3 %all-gather.17.cloned.1.call-done = bf16[512,2048]{1,0:T(8,128)(2,1)} async-done(((bf16[128,2048]{1,0:T(8,128)(2,1)}), bf16[512,2048]{1,0:T(8,128)(2,1)}) %all-gather.17.cloned.1.call-update) | async-done | bytes 2097168 | tf_op jit(solution)/shard_map/all_gather | solution.py:277
  735.7 4.2 convolution_convert_fusion.3
  740.0 3.7 convolution_convert_fusion.6
  745.6 3.4 multiply_reduce_fusion
  756.7 9.5 bitcast_convert_fusion
  766.5 6.9 convert_bitcast_fusion.1
  773.5 19.1 %convolution_convert_fusion.2 = bf16[2048,1408]{1,0:T(8,128)(2,1)} fusion(bf16[2048,2048]{1,0:T(8,128)(2,1)} %all-gather.13.cloned.1.call-done, bf16[2048,704]{0,1:T(8,128)(2,1)} %copy-done.63, bf16[2048,704]{0,1:T(8,128)(2,1)} %copy-done.62), kind=kOutput, calls=%fused_computation.4 | convolution fusion | flops 11825577984 | bytes 19922944 | tf_op jit(solution)/shard_map/dot_general | solution.py:64
  792.6 8.3 copy.243
  800.9 5.6 all-to-all-start.5
  806.8 11.0 %convolution_bitcast_fusion = f32[1,704,2048]{2,1,0:T(8,128)} fusion(bf16[2048,704]{0,1:T(8,128)(2,1)} %copy-done.22, bf16[2048,2048]{1,0:T(8,128)(2,1)} %all-gather.15.cloned.1.call-done), kind=kOutput, calls=%fused_computation.26 | convolution fusion | flops 5905580032 | bytes 17039360 | tf_op jit(solution)/shard_map/dot_general | solution.py:64
  817.8 67.3 %all-to-all-done.5 = bf16[8,256,1408]{1,2,0:T(8,128)(2,1)} async-done(((bf16[8,256,1408]{1,2,0:T(8,128)(2,1)}), bf16[8,256,1408]{1,2,0:T(8,128)(2,1)}, u32[]{:S(2)}, u32[]{:S(2)}) %all-to-all-start.5) | async-done | bytes 5767200 | tf_op jit(solution)/shard_map/all_to_all | solution.py:99
  885.1 8.3 convert_bitcast_fusion
  893.4 10.1 %copy.244 = f32[256,2,8,704]{0,3,2,1:T(8,128)} copy(f32[256,2,8,704]{0,3,1,2:T(8,128)} %convert_bitcast_fusion) | data formatting | bytes 23068672 | tf_op jit(solution)/shard_map/convert_element_type | solution.py:101
  903.5 12.0 %copy.246 = f32[1,256,11264]{2,1,0:T(8,128)} copy(f32[1,256,11264]{1,2,0:T(8,128)} %bitcast.118) | data formatting | bytes 23068672
  915.4 2.8 fusion.3
  918.3 43.9 %psum.7 = f32[6,2048]{1,0:T(8,128)S(1)} all-reduce(f32[6,2048]{1,0:T(8,128)S(1)} %pad_maximum_fusion.14), channel_id=1, replica_groups=mesh['dp'=8,'expert'=4] {'dp','expert'}, use_global_device_ids=true, to_apply=%region_24.25 | all-reduce | flops 12288 | bytes 98304 | tf_op jit(solution)/shard_map/psum | solution.py:322
  963.6 1.8 convert_element_type.238
  965.3 1.4 fusion.26
  966.8 4.4 fusion.30
  971.2 2.6 copy.245
  (222 shorter events, 36.1 us)
Async XLA Ops:
  7.2 348.5 %copy-start = (bf16[1,704,2048]{2,1,0:T(8,128)(2,1)S(1)}, bf16[1,704,2048]{2,1,0:T(8,128)(2,1)}, u32[]{:S(2)}) copy-start(bf16[1,704,2048]{2,1,0:T(8,128)(2,1)} %param.19) | copy-start | bytes 8650756
  7.2 47.9 %all-gather.7.cloned.1.call-start = ((), (), s32[]{:S(2)}) async-start(), calls=%async_computation.12 | async-start | bytes 2621440 | tf_op jit(solution)/shard_map/all_gather | solution.py:175
  7.9 96.6 %all-gather.9.cloned.1.call-start = ((), (), s32[]{:S(2)}) async-start(), calls=%async_computation.13 | async-start | bytes 7077888 | tf_op jit(solution)/shard_map/all_gather | solution.py:178
  10.4 124.3 %all-gather.11.cloned.1.call-start = ((), (), s32[]{:S(2)}) async-start(), calls=%async_computation.14 | async-start | bytes 2359296 | tf_op jit(solution)/shard_map/all_gather | solution.py:179
  11.1 169.8 %reduce-scatter.7.cloned.1.call-start = ((), (), s32[]{:S(2)}) async-start(), calls=%async_computation.15 | async-start | bytes 2621440 | tf_op jit(solution)/shard_map/reduce_scatter | solution.py:217
  22.9 88.1 %copy-start.29 = (bf16[2048,6]{0,1:T(8,128)(2,1)}, bf16[2048,6]{0,1:T(8,128)(2,1)S(1)}, u32[]{:S(2)}) copy-start(bf16[2048,6]{0,1:T(8,128)(2,1)S(1)} %all_gather.22) | copy-start | bytes 73732
  22.9 88.0 %copy-start.35 = (f32[2048,1]{0,1:T(1,128)}, f32[2048,1]{0,1:T(1,128)S(1)}, u32[]{:S(2)}) copy-start(f32[2048,1]{0,1:T(1,128)S(1)} %get-tuple-element.99) | copy-start | bytes 24580
  22.9 159.3 %copy-start.31 = (f32[2048,1]{0,1:T(1,128)}, f32[2048,1]{0,1:T(1,128)S(1)}, u32[]{:S(2)}) copy-start(f32[2048,1]{0,1:T(1,128)S(1)} %get-tuple-element.98) | copy-start | bytes 24580
  57.2 53.8 %copy-start.44 = (f32[512]{0:T(512)}, f32[512]{0:T(512)S(1)}, u32[]{:S(2)}) copy-start(f32[512]{0:T(512)S(1)} %add_rsqrt_fusion) | copy-start | bytes 6148
  124.5 3.3 copy-start.27
  127.8 2.1 copy-start.14
  127.8 3.5 copy-start.25
  129.2 2.1 copy-start.2
  129.2 2.1 copy-start.33
  133.0 6.9 copy-start.60
  133.0 7.2 copy-start.39
  134.7 46.2 %copy-start.5 = (bf16[128,2048]{1,0:T(8,128)(2,1)S(1)}, bf16[128,2048]{1,0:T(8,128)(2,1)}, u32[]{:S(2)}) copy-start(bf16[128,2048]{1,0:T(8,128)(2,1)} %param.12) | copy-start | bytes 1572868
  139.1 190.8 %all-gather.13.cloned.1.call-start = ((), (), s32[]{:S(2)}) async-start(), calls=%async_computation.16 | async-start | bytes 9437184 | tf_op jit(solution)/shard_map/all_gather | solution.py:124
  141.0 39.9 %copy-start.48 = (pred[128,2]{0,1:T(4,128)(4,1)}, pred[128,2]{0,1:T(4,128)(4,1)S(1)}, u32[]{:S(2)}) copy-start(pred[128,2]{0,1:T(4,128)(4,1)S(1)} %copy.223) | copy-start | bytes 772
  182.2 41.1 %copy-start.46 = (f32[128]{0:T(128)}, f32[128]{0:T(128)S(1)}, u32[]{:S(2)}) copy-start(f32[128]{0:T(128)S(1)} %add_rsqrt_fusion.2) | copy-start | bytes 1540
  214.7 221.4 %reduce-scatter.9.cloned.1.call-start = ((), (), s32[]{:S(2)}) async-start(), calls=%async_computation.17 | async-start | bytes 9437184 | tf_op jit(solution)/shard_map/reduce_scatter | solution.py:127
  436.1 27.6 %all-to-all-start.2 = ((bf16[4,64,2048]{2,1,0:T(8,128)(2,1)}), bf16[4,64,2048]{2,1,0:T(8,128)(2,1)}, u32[]{:S(2)}, u32[]{:S(2)}) async-start(bf16[4,64,2048]{2,1,0:T(8,128)(2,1)} %bitcast.138), calls=%async_computation.4 | async-start | bytes 2097152 | tf_op jit(solution)/shard_map/all_to_all | solution.py:81
  441.2 114.1 %all-gather.15.cloned.1.call-start = ((), (), s32[]{:S(2)}) async-start(), calls=%async_computation.18 | async-start | bytes 9437184 | tf_op jit(solution)/shard_map/all_gather | solution.py:125
  446.3 23.9 %copy-start.40 = (f32[128]{0:T(128)S(1)}, f32[128]{0:T(128)}, u32[]{:S(2)}) copy-start(f32[128]{0:T(128)} %get-tuple-element.70) | copy-start | bytes 1540
  449.3 19.8 %copy-start.57 = (f32[128]{0:T(128)}, f32[128]{0:T(128)S(1)}, u32[]{:S(2)}) copy-start(f32[128]{0:T(128)S(1)} %get-tuple-element.72) | copy-start | bytes 1540
  463.7 5.4 copy-start.59
  463.7 6.6 copy-start.6
  470.2 31.1 %copy-start.42 = (f32[128,2]{0,1:T(2,128)}, f32[128,2]{0,1:T(2,128)S(1)}, u32[]{:S(2)}) copy-start(f32[128,2]{0,1:T(2,128)S(1)} %get-tuple-element.69) | copy-start | bytes 3076
  470.2 31.1 %copy-start.49 = (f32[128]{0:T(128)}, f32[128]{0:T(128)S(1)}, u32[]{:S(2)}) copy-start(f32[128]{0:T(128)S(1)} %get-tuple-element.100) | copy-start | bytes 1540
  470.2 31.1 %copy-start.51 = (f32[128]{0:T(128)}, f32[128]{0:T(128)S(1)}, u32[]{:S(2)}) copy-start(f32[128]{0:T(128)S(1)} %get-tuple-element.101) | copy-start | bytes 1540
  501.3 158.7 %reduce-scatter.11.cloned.1.call-start = ((), (), s32[]{:S(2)}) async-start(), calls=%async_computation.19 | async-start | bytes 9437184 | tf_op jit(solution)/shard_map/reduce_scatter | solution.py:128
  568.5 2.5 copy-start.63
  588.6 76.7 %copy-start.43 = (f32[128,2]{0,1:T(2,128)S(1)}, f32[128,2]{0,1:T(2,128)}, u32[]{:S(2)}) copy-start(f32[128,2]{0,1:T(2,128)} %copy-done.42) | copy-start | bytes 3076
  588.6 76.7 %copy-start.54 = (f32[128]{0:T(128)S(1)}, f32[128]{0:T(128)}, u32[]{:S(2)}) copy-start(f32[128]{0:T(128)} %copy-done.53) | copy-start | bytes 1540
  588.6 76.7 %copy-start.56 = (f32[128]{0:T(128)S(1)}, f32[128]{0:T(128)}, u32[]{:S(2)}) copy-start(f32[128]{0:T(128)} %copy-done.55) | copy-start | bytes 1540
  588.6 76.7 %copy-start.58 = (f32[128]{0:T(128)S(1)}, f32[128]{0:T(128)}, u32[]{:S(2)}) copy-start(f32[128]{0:T(128)} %get-tuple-element.68) | copy-start | bytes 1540
  588.6 99.3 %copy-start.8 = (bf16[128,2048]{1,0:T(8,128)(2,1)S(1)}, bf16[128,2048]{1,0:T(8,128)(2,1)}, u32[]{:S(2)}) copy-start(bf16[128,2048]{1,0:T(8,128)(2,1)} %reduce-scatter.7.cloned.1.call-done) | copy-start | bytes 1572868
  588.7 99.3 %copy-start.30 = (bf16[2048,6]{0,1:T(8,128)(2,1)S(1)}, bf16[2048,6]{0,1:T(8,128)(2,1)}, u32[]{:S(2)}) copy-start(bf16[2048,6]{0,1:T(8,128)(2,1)} %copy-done.29) | copy-start | bytes 73732
  588.7 99.3 %copy-start.32 = (f32[2048,1]{0,1:T(1,128)S(1)}, f32[2048,1]{0,1:T(1,128)}, u32[]{:S(2)}) copy-start(f32[2048,1]{0,1:T(1,128)} %copy-done.31) | copy-start | bytes 24580
  588.7 99.3 %copy-start.47 = (f32[128]{0:T(128)S(1)}, f32[128]{0:T(128)}, u32[]{:S(2)}) copy-start(f32[128]{0:T(128)} %copy-done.46) | copy-start | bytes 1540
  588.7 100.3 %copy-start.7 = (bf16[128,2048]{1,0:T(8,128)(2,1)S(1)}, bf16[128,2048]{1,0:T(8,128)(2,1)}, u32[]{:S(2)}) copy-start(bf16[128,2048]{1,0:T(8,128)(2,1)} %param.23) | copy-start | bytes 1572868
  588.7 100.3 %copy-start.41 = (f32[128]{0:T(128)S(1)}, f32[128]{0:T(128)}, u32[]{:S(2)}) copy-start(f32[128]{0:T(128)} %get-tuple-element.70) | copy-start | bytes 1540
  660.0 27.6 %all-to-all-start.4 = ((bf16[4,64,2048]{2,1,0:T(8,128)(2,1)}), bf16[4,64,2048]{2,1,0:T(8,128)(2,1)S(1)}, u32[]{:S(2)}, u32[]{:S(2)}) async-start(bf16[4,64,2048]{2,1,0:T(8,128)(2,1)} %bitcast.139), calls=%async_computation.7 | async-start | bytes 2097152 | tf_op jit(solution)/shard_map/all_to_all | solution.py:81
  665.1 70.6 %all-gather.17.cloned.1.call-start = ((), (), s32[]{:S(2)}) async-start(), calls=%async_computation.20 | async-start | bytes 2621440 | tf_op jit(solution)/shard_map/all_gather | solution.py:277
  687.6 2.8 copy-start.34
  687.6 2.8 copy-start.38
  687.6 48.1 %copy-start.61 = (bf16[4,128,512]{2,1,0:T(8,128)(2,1)S(1)}, bf16[4,128,512]{2,1,0:T(8,128)(2,1)}, u32[]{:S(2)}) copy-start(bf16[4,128,512]{2,1,0:T(8,128)(2,1)} %fusion.21) | copy-start | bytes 1572868
  689.0 50.9 %copy-start.10 = (f32[128,2048]{1,0:T(8,128)}, f32[128,2048]{1,0:T(8,128)S(1)}, u32[]{:S(2)}) copy-start(f32[128,2048]{1,0:T(8,128)S(1)} %get-tuple-element.107) | copy-start | bytes 3145732
  690.3 273.3 %reduce-scatter.17.cloned.1.call-start = ((), (), s32[]{:S(2)}) async-start(), calls=%async_computation.23 | async-start | bytes 2359296 | tf_op jit(solution)/shard_map/reduce_scatter | solution.py:280
  740.0 225.4 %reduce-scatter.13.cloned.1.call-start = ((), (), s32[]{:S(2)}) async-start(), calls=%async_computation.21 | async-start | bytes 2621440 | tf_op jit(solution)/shard_map/reduce_scatter | solution.py:305
  740.0 3.7 copy-start.3
  745.6 3.8 copy-start.4
  750.6 2.3 copy-start.23
  750.6 2.3 copy-start.24
  756.7 9.8 copy-start.11
  756.7 9.8 copy-start.28
  756.7 9.8 copy-start.36
  756.7 9.8 copy-start.45
  766.2 205.0 %reduce-scatter.15.cloned.1.call-start = ((), (), s32[]{:S(2)}) async-start(), calls=%async_computation.22 | async-start | bytes 7077888 | tf_op jit(solution)/shard_map/reduce_scatter | solution.py:309
  800.9 5.6 copy-start.13
  800.9 84.2 %all-to-all-start.5 = ((bf16[8,256,1408]{1,2,0:T(8,128)(2,1)}), bf16[8,256,1408]{1,2,0:T(8,128)(2,1)}, u32[]{:S(2)}, u32[]{:S(2)}) async-start(bf16[8,256,1408]{1,2,0:T(8,128)(2,1)} %copy.243), calls=%async_computation.11 | async-start | bytes 11534336 | tf_op jit(solution)/shard_map/all_to_all | solution.py:99
  915.4 51.3 %copy-start.50 = (f32[128]{0:T(128)S(1)}, f32[128]{0:T(128)}, u32[]{:S(2)}) copy-start(f32[128]{0:T(128)} %copy-done.49) | copy-start | bytes 1540
  915.4 51.3 %copy-start.52 = (f32[128]{0:T(128)S(1)}, f32[128]{0:T(128)}, u32[]{:S(2)}) copy-start(f32[128]{0:T(128)} %copy-done.51) | copy-start | bytes 1540
  966.7 7.0 copy-start.1
  (15 other events, 22.7 us)
Sparse Core Ops, SparseCore 0:
  9.6 45.4 all-gather.6
  57.5 46.9 all-gather.8
  106.5 28.1 all-gather.10
  139.2 41.6 reduce-scatter.6
  214.9 108.8 all-gather.12
  364.9 71.1 reduce-scatter.8
  501.4 53.8 all-gather.14
  588.8 71.1 reduce-scatter.10
  690.4 45.2 all-gather.16
  740.1 41.5 reduce-scatter.16
  784.0 41.6 reduce-scatter.12
  829.2 76.9 reduce-scatter.14
where the time goes:
time: 991 us; the launch traced here: 981 us
  waiting for transfers between devices  465 us (47%)
  blocking collectives  208 us (21%)
  matrix products  142 us (14%)
  local copies, waits for them, and re-layouts  89.1 us (9%)
  other arithmetic  43.6 us (4%)
  starting transfers between devices  17.2 us (2%)
  between operations  16.3 us (2%)
    all_to_all x1, blocking collectives, by_hidden(): got = lax.all_to_all(pieces, 'dp', split_axis=0, concat_axis=0, tiled=True)  94.9 us
    reduce_scatter x1, waiting for transfers between devices, experts_split_hidden(): out = lax.psum_scatter(out, 'dp', scatter_dimension=0, tiled=True)  71.4 us
    reduce_scatter x1, waiting for transfers between devices, experts_split_hidden(): d_rows = lax.psum_scatter(d_rows, 'dp', scatter_dimension=0, tiled=True)  71.3 us
    all_to_all x1, waiting for transfers between devices, by_rows(): got = lax.all_to_all(pieces, 'dp', split_axis=0, concat_axis=0, tiled=True)  67.3 us
    all_to_all x2, blocking collectives, exchange_experts(): lax.all_to_all(blocks, 'expert', split_axis=0, concat_axis=0, tiled=True)  59.9 us
    all_gather x1, waiting for transfers between devices, experts_split_hidden(): all_d_out = lax.all_gather(d_rows_out, 'dp', axis=0, tiled=True)  54 us
    all_gather x1, waiting for transfers between devices, on_device(): qkv_full = lax.all_gather(w_qkv, 'dp', axis=1, tiled=True)  47.4 us
    all_gather x1, waiting for transfers between devices, on_device(): whole_grad = lax.all_gather(d_attn, 'expert', axis=0, tiled=True)  45.3 us
  transfers between devices with their start and end apart: 15, of which 11 were waited for; matrix products, arithmetic and copies ran while one was open for 18% of the time, Pallas kernels for 0%

commit v1 on v0

--- a/solution.py
+++ b/solution.py
@@ -319,7 +319,7 @@
     small_part = jnp.concatenate(
         [first_gain_part[None], gain_two_part[None], router_part.T], axis=0
     )
-    small_sum = lax.psum(small_part, ("dp", "expert"))
+    small_sum = lax.psum(lax.psum(small_part, "expert"), "dp")
     own_rows = width // dp_size
     small_own = lax.dynamic_slice_in_dim(
         small_sum, lax.axis_index("dp") * own_rows, own_rows, axis=1

time: 991 us -> 992 us (level)
    psum x1 -> x2, blocking collectives: 43.9 us -> 39.8 us  [on_device(): small_sum = lax.psum(lax.psum(small_part, 'expert'), 'dp')]
where the time goes in v1:
time: 992 us; the launch traced here: 977 us
  waiting for transfers between devices  465 us (47%)
  blocking collectives  204 us (21%)
  matrix products  142 us (14%)
  local copies, waits for them, and re-layouts  89.1 us (9%)
  other arithmetic  43.7 us (4%)
  starting transfers between devices  17.2 us (2%)
  between operations  16.3 us (2%)
    all_to_all x1, blocking collectives, by_hidden(): got = lax.all_to_all(pieces, 'dp', split_axis=0, concat_axis=0, tiled=True)  94.9 us
    reduce_scatter x1, waiting for transfers between devices, experts_split_hidden(): out = lax.psum_scatter(out, 'dp', scatter_dimension=0, tiled=True)  71.3 us
    reduce_scatter x1, waiting for transfers between devices, experts_split_hidden(): d_rows = lax.psum_scatter(d_rows, 'dp', scatter_dimension=0, tiled=True)  71.3 us
    all_to_all x1, waiting for transfers between devices, by_rows(): got = lax.all_to_all(pieces, 'dp', split_axis=0, concat_axis=0, tiled=True)  67.3 us
    all_to_all x2, blocking collectives, exchange_experts(): lax.all_to_all(blocks, 'expert', split_axis=0, concat_axis=0, tiled=True)  59.9 us
    all_gather x1, waiting for transfers between devices, experts_split_hidden(): all_d_out = lax.all_gather(d_rows_out, 'dp', axis=0, tiled=True)  54 us
    all_gather x1, waiting for transfers between devices, on_device(): qkv_full = lax.all_gather(w_qkv, 'dp', axis=1, tiled=True)  47.4 us
    all_gather x1, waiting for transfers between devices, on_device(): whole_grad = lax.all_gather(d_attn, 'expert', axis=0, tiled=True)  45.3 us
  transfers between devices with their start and end apart: 15, of which 11 were waited for; matrix products, arithmetic and copies ran while one was open for 18% of the time, Pallas kernels for 0%

profile of v1, /device:TPU:10, one launch (start us, length us, event | category | flops | bytes accessed | tf_op | source)
XLA Modules:
  0.0 976.8 jit_solution(420965412824298991)
XLA Ops:
  8.0 2.4 copy.213
  13.8 9.1 all_gather.22
  23.8 1.7 fusion.41
  25.5 29.6 %all-gather.7.cloned.1.call-done = bf16[512,2048]{1,0:T(8,128)(2,1)} async-done(((bf16[128,2048]{1,0:T(8,128)(2,1)}), bf16[512,2048]{1,0:T(8,128)(2,1)}) %all-gather.7.cloned.1.call-update) | async-done | bytes 2097168 | tf_op jit(solution)/shard_map/all_gather | solution.py:175
  55.1 2.1 fusion.4
  57.2 47.4 %all-gather.9.cloned.1.call-done = bf16[3,2048,512]{1,2,0:T(8,128)(2,1)} async-done(((bf16[3,256,512]{1,2,0:T(8,128)(2,1)}), bf16[3,2048,512]{1,2,0:T(8,128)(2,1)}) %all-gather.9.cloned.1.call-update) | async-done | bytes 6291472 | tf_op jit(solution)/shard_map/all_gather | solution.py:178
  104.6 6.4 convolution_bitcast_fusion.1
  113.9 2.4 copy.260
  116.2 2.2 fusion.66
  118.5 2.4 copy.262
  120.8 1.3 copy.259
  122.1 2.4 copy.261
  124.5 3.3 subtract_convert_fusion.3
  127.8 1.4 fusion.68
  129.9 1.4 copy-done.2
  131.3 1.7 fusion.21
  133.0 1.7 all-gather.11.cloned.1.call-done
  134.7 4.4 convolution_convert_fusion.4
  141.3 39.5 %reduce-scatter.7.cloned.1.call-done = bf16[128,2048]{1,0:T(8,128)(2,1)} async-done(((bf16[512,2048]{1,0:T(8,128)(2,1)}), bf16[128,2048]{1,0:T(8,128)(2,1)}) %reduce-scatter.7.cloned.1.call-update) | async-done | bytes 524304 | tf_op jit(solution)/shard_map/reduce_scatter | solution.py:217
  184.7 30.0 %all_to_all.30 = bf16[4,64,2048]{2,1,0:T(8,128)(2,1)} all-to-all(bf16[4,64,2048]{2,1,0:T(8,128)(2,1)S(1)} %bitcast.127), channel_id=1, replica_groups=mesh['dp'=8,'expert'=4] {'expert'}, dimensions={0} | all-to-all | bytes 2097152 | tf_op jit(solution)/shard_map/all_to_all | solution.py:81
  214.9 8.4 copy.224
  223.3 3.4 copy.225
  226.8 94.9 %all_to_all.31 = bf16[8,256,1408]{1,2,0:T(8,128)(2,1)} all-to-all(bf16[8,256,1408]{1,2,0:T(8,128)(2,1)S(1)} %bitcast.119), channel_id=1, replica_groups=mesh['dp'=8,'expert'=4] {'dp'}, dimensions={0} | all-to-all | bytes 11534336 | tf_op jit(solution)/shard_map/all_to_all | solution.py:90
  321.6 8.2 copy.226
  329.9 18.8 %fusion.69 = f32[2048,1408]{0,1:T(8,128)} fusion(bf16[2048,2048]{1,0:T(8,128)(2,1)} %all-gather.13.cloned.1.call-done, bf16[2048,1408]{1,0:T(8,128)(2,1)} %bitcast.121), kind=kOutput, calls=%fused_computation.161 | convolution fusion | flops 11811160064 | bytes 25690112 | tf_op jit(solution)/shard_map/dot_general | solution.py:106
  348.7 5.2 multiply_convert_fusion.2
  354.0 1.7 copy-done.22
  355.6 9.1 convolution_convert_fusion.1
  364.7 71.3 %reduce-scatter.9.cloned.1.call-done = bf16[256,2048]{1,0:T(8,128)(2,1)} async-done(((bf16[2048,2048]{1,0:T(8,128)(2,1)}), bf16[256,2048]{1,0:T(8,128)(2,1)}) %reduce-scatter.9.cloned.1.call-update) | async-done | bytes 1048592 | tf_op jit(solution)/shard_map/reduce_scatter | solution.py:127
  436.1 5.1 all-to-all-start.2
  443.9 2.4 gather_fusion
  447.1 1.5 copy.220
  449.8 13.9 %all-to-all-done.2 = bf16[4,64,2048]{2,1,0:T(8,128)(2,1)} async-done(((bf16[4,64,2048]{2,1,0:T(8,128)(2,1)}), bf16[4,64,2048]{2,1,0:T(8,128)(2,1)}, u32[]{:S(2)}, u32[]{:S(2)}) %all-to-all-start.2) | async-done | bytes 1048608 | tf_op jit(solution)/shard_map/all_to_all | solution.py:81
  463.7 1.6 fusion.44
  466.3 2.8 multiply_reduce_fusion.4
  471.4 29.9 %all_to_all.32 = bf16[4,64,2048]{2,1,0:T(8,128)(2,1)} all-to-all(bf16[4,64,2048]{2,1,0:T(8,128)(2,1)S(1)} %bitcast.130), channel_id=1, replica_groups=mesh['dp'=8,'expert'=4] {'expert'}, dimensions={0} | all-to-all | bytes 2097152 | tf_op jit(solution)/shard_map/all_to_all | solution.py:81
  501.4 54.0 %all-gather.15.cloned.1.call-done = bf16[2048,2048]{1,0:T(8,128)(2,1)} async-done(((bf16[256,2048]{1,0:T(8,128)(2,1)}), bf16[2048,2048]{1,0:T(8,128)(2,1)}) %all-gather.15.cloned.1.call-update) | async-done | bytes 8388624 | tf_op jit(solution)/shard_map/all_gather | solution.py:125
  555.4 13.1 %multiply_convert_fusion.1 = (bf16[2048,704]{0,1:T(8,128)(2,1)S(1)}, bf16[2048,704]{0,1:T(8,128)(2,1)S(1)}) fusion(f32[2048,1408]{0,1:T(8,128)} %fusion.69, bf16[2048,2048]{1,0:T(8,128)(2,1)} %all-gather.15.cloned.1.call-done, bf16[1,704,2048]{2,1,0:T(8,128)(2,1)S(1)} %copy-done), kind=kOutput, calls=%fused_computation.8 | convolution fusion | flops 5924323328 | bytes 28573696 | tf_op jit(solution)/shard_map/dot_general | solution.py:70
  568.5 1.5 copy-done.62
  570.9 17.7 %convolution_convert_fusion = bf16[2048,2048]{1,0:T(8,128)(2,1)} fusion(bf16[2048,1408]{1,0:T(8,128)(2,1)} %bitcast.122, bf16[2048,704]{0,1:T(8,128)(2,1)S(1)} %get-tuple-element.75, bf16[2048,704]{0,1:T(8,128)(2,1)S(1)} %get-tuple-element.74), kind=kOutput, calls=%fused_computation.2 | convolution fusion | flops 11826888704 | bytes 19922944 | tf_op jit(solution)/shard_map/dot_general | solution.py:70
  588.7 71.3 %reduce-scatter.11.cloned.1.call-done = bf16[256,2048]{1,0:T(8,128)(2,1)} async-done(((bf16[2048,2048]{1,0:T(8,128)(2,1)}), bf16[256,2048]{1,0:T(8,128)(2,1)}) %reduce-scatter.11.cloned.1.call-update) | async-done | bytes 1048592 | tf_op jit(solution)/shard_map/reduce_scatter | solution.py:128
  660.0 5.1 all-to-all-start.4
  665.3 22.2 %all-to-all-done.4 = bf16[4,64,2048]{2,1,0:T(8,128)(2,1)S(1)} async-done(((bf16[4,64,2048]{2,1,0:T(8,128)(2,1)}), bf16[4,64,2048]{2,1,0:T(8,128)(2,1)S(1)}, u32[]{:S(2)}, u32[]{:S(2)}) %all-to-all-start.4) | async-done | bytes 1048608 | tf_op jit(solution)/shard_map/all_to_all | solution.py:81
  690.3 45.3 %all-gather.17.cloned.1.call-done = bf16[512,2048]{1,0:T(8,128)(2,1)} async-done(((bf16[128,2048]{1,0:T(8,128)(2,1)}), bf16[512,2048]{1,0:T(8,128)(2,1)}) %all-gather.17.cloned.1.call-update) | async-done | bytes 2097168 | tf_op jit(solution)/shard_map/all_gather | solution.py:277
  735.7 4.2 convolution_convert_fusion.3
  740.0 3.7 convolution_convert_fusion.6
  745.5 3.4 multiply_reduce_fusion
  756.7 9.5 bitcast_convert_fusion
  766.5 6.9 convert_bitcast_fusion.1
  773.4 19.1 %convolution_convert_fusion.2 = bf16[2048,1408]{1,0:T(8,128)(2,1)} fusion(bf16[2048,2048]{1,0:T(8,128)(2,1)} %all-gather.13.cloned.1.call-done, bf16[2048,704]{0,1:T(8,128)(2,1)} %copy-done.63, bf16[2048,704]{0,1:T(8,128)(2,1)} %copy-done.62), kind=kOutput, calls=%fused_computation.4 | convolution fusion | flops 11825577984 | bytes 19922944 | tf_op jit(solution)/shard_map/dot_general | solution.py:64
  792.5 8.3 copy.243
  800.8 5.6 all-to-all-start.5
  806.7 11.0 %convolution_bitcast_fusion = f32[1,704,2048]{2,1,0:T(8,128)} fusion(bf16[2048,704]{0,1:T(8,128)(2,1)} %copy-done.22, bf16[2048,2048]{1,0:T(8,128)(2,1)} %all-gather.15.cloned.1.call-done), kind=kOutput, calls=%fused_computation.26 | convolution fusion | flops 5905580032 | bytes 17039360 | tf_op jit(solution)/shard_map/dot_general | solution.py:64
  817.7 67.3 %all-to-all-done.5 = bf16[8,256,1408]{1,2,0:T(8,128)(2,1)} async-done(((bf16[8,256,1408]{1,2,0:T(8,128)(2,1)}), bf16[8,256,1408]{1,2,0:T(8,128)(2,1)}, u32[]{:S(2)}, u32[]{:S(2)}) %all-to-all-start.5) | async-done | bytes 5767200 | tf_op jit(solution)/shard_map/all_to_all | solution.py:99
  885.0 8.3 convert_bitcast_fusion
  893.4 10.1 %copy.244 = f32[256,2,8,704]{0,3,2,1:T(8,128)} copy(f32[256,2,8,704]{0,3,1,2:T(8,128)} %convert_bitcast_fusion) | data formatting | bytes 23068672 | tf_op jit(solution)/shard_map/convert_element_type | solution.py:101
  903.4 12.0 %copy.246 = f32[1,256,11264]{2,1,0:T(8,128)} copy(f32[1,256,11264]{1,2,0:T(8,128)} %bitcast.118) | data formatting | bytes 23068672
  915.4 2.8 fusion.3
  918.3 17.2 %psum.14 = f32[6,2048]{1,0:T(8,128)S(1)} all-reduce(f32[6,2048]{1,0:T(8,128)S(1)} %pad_maximum_fusion.14), channel_id=1, replica_groups=mesh['dp'=8,'expert'=4] {'expert'}, use_global_device_ids=true, to_apply=%region_24.25 | all-reduce | flops 12288 | bytes 98304 | tf_op jit(solution)/shard_map/psum | solution.py:322
  935.5 22.6 %psum.15 = f32[6,2048]{1,0:T(8,128)S(1)} all-reduce(f32[6,2048]{1,0:T(8,128)S(1)} %psum.14), channel_id=1, replica_groups=mesh['dp'=8,'expert'=4] {'dp'}, use_global_device_ids=true, to_apply=%region_25.26 | all-reduce | flops 12288 | bytes 98304 | tf_op jit(solution)/shard_map/psum | solution.py:322
  959.3 1.8 convert_element_type.238
  961.1 1.4 fusion.26
  962.5 4.4 fusion.30
  967.0 2.6 copy.245
  (223 shorter events, 37.4 us)
Async XLA Ops:
  7.2 348.5 %copy-start = (bf16[1,704,2048]{2,1,0:T(8,128)(2,1)S(1)}, bf16[1,704,2048]{2,1,0:T(8,128)(2,1)}, u32[]{:S(2)}) copy-start(bf16[1,704,2048]{2,1,0:T(8,128)(2,1)} %param.19) | copy-start | bytes 8650756
  7.2 47.9 %all-gather.7.cloned.1.call-start = ((), (), s32[]{:S(2)}) async-start(), calls=%async_computation.12 | async-start | bytes 2621440 | tf_op jit(solution)/shard_map/all_gather | solution.py:175
  7.9 96.6 %all-gather.9.cloned.1.call-start = ((), (), s32[]{:S(2)}) async-start(), calls=%async_computation.13 | async-start | bytes 7077888 | tf_op jit(solution)/shard_map/all_gather | solution.py:178
  10.4 124.3 %all-gather.11.cloned.1.call-start = ((), (), s32[]{:S(2)}) async-start(), calls=%async_computation.14 | async-start | bytes 2359296 | tf_op jit(solution)/shard_map/all_gather | solution.py:179
  11.1 169.8 %reduce-scatter.7.cloned.1.call-start = ((), (), s32[]{:S(2)}) async-start(), calls=%async_computation.15 | async-start | bytes 2621440 | tf_op jit(solution)/shard_map/reduce_scatter | solution.py:217
  22.9 88.1 %copy-start.29 = (bf16[2048,6]{0,1:T(8,128)(2,1)}, bf16[2048,6]{0,1:T(8,128)(2,1)S(1)}, u32[]{:S(2)}) copy-start(bf16[2048,6]{0,1:T(8,128)(2,1)S(1)} %all_gather.22) | copy-start | bytes 73732
  22.9 88.0 %copy-start.35 = (f32[2048,1]{0,1:T(1,128)}, f32[2048,1]{0,1:T(1,128)S(1)}, u32[]{:S(2)}) copy-start(f32[2048,1]{0,1:T(1,128)S(1)} %get-tuple-element.99) | copy-start | bytes 24580
  22.9 159.3 %copy-start.31 = (f32[2048,1]{0,1:T(1,128)}, f32[2048,1]{0,1:T(1,128)S(1)}, u32[]{:S(2)}) copy-start(f32[2048,1]{0,1:T(1,128)S(1)} %get-tuple-element.98) | copy-start | bytes 24580
  57.2 53.8 %copy-start.44 = (f32[512]{0:T(512)}, f32[512]{0:T(512)S(1)}, u32[]{:S(2)}) copy-start(f32[512]{0:T(512)S(1)} %add_rsqrt_fusion) | copy-start | bytes 6148
  124.5 3.3 copy-start.27
  127.8 2.0 copy-start.14
  127.8 3.4 copy-start.25
  129.2 2.1 copy-start.2
  129.2 2.0 copy-start.33
  133.0 7.0 copy-start.60
  133.0 7.2 copy-start.39
  134.7 46.2 %copy-start.5 = (bf16[128,2048]{1,0:T(8,128)(2,1)S(1)}, bf16[128,2048]{1,0:T(8,128)(2,1)}, u32[]{:S(2)}) copy-start(bf16[128,2048]{1,0:T(8,128)(2,1)} %param.12) | copy-start | bytes 1572868
  139.1 190.7 %all-gather.13.cloned.1.call-start = ((), (), s32[]{:S(2)}) async-start(), calls=%async_computation.16 | async-start | bytes 9437184 | tf_op jit(solution)/shard_map/all_gather | solution.py:124
  141.0 39.8 %copy-start.48 = (pred[128,2]{0,1:T(4,128)(4,1)}, pred[128,2]{0,1:T(4,128)(4,1)S(1)}, u32[]{:S(2)}) copy-start(pred[128,2]{0,1:T(4,128)(4,1)S(1)} %copy.223) | copy-start | bytes 772
  182.2 41.2 %copy-start.46 = (f32[128]{0:T(128)}, f32[128]{0:T(128)S(1)}, u32[]{:S(2)}) copy-start(f32[128]{0:T(128)S(1)} %add_rsqrt_fusion.2) | copy-start | bytes 1540
  214.7 221.4 %reduce-scatter.9.cloned.1.call-start = ((), (), s32[]{:S(2)}) async-start(), calls=%async_computation.17 | async-start | bytes 9437184 | tf_op jit(solution)/shard_map/reduce_scatter | solution.py:127
  436.1 27.6 %all-to-all-start.2 = ((bf16[4,64,2048]{2,1,0:T(8,128)(2,1)}), bf16[4,64,2048]{2,1,0:T(8,128)(2,1)}, u32[]{:S(2)}, u32[]{:S(2)}) async-start(bf16[4,64,2048]{2,1,0:T(8,128)(2,1)} %bitcast.138), calls=%async_computation.4 | async-start | bytes 2097152 | tf_op jit(solution)/shard_map/all_to_all | solution.py:81
  441.2 114.2 %all-gather.15.cloned.1.call-start = ((), (), s32[]{:S(2)}) async-start(), calls=%async_computation.18 | async-start | bytes 9437184 | tf_op jit(solution)/shard_map/all_gather | solution.py:125
  446.3 23.9 %copy-start.40 = (f32[128]{0:T(128)S(1)}, f32[128]{0:T(128)}, u32[]{:S(2)}) copy-start(f32[128]{0:T(128)} %get-tuple-element.70) | copy-start | bytes 1540
  449.2 19.8 %copy-start.57 = (f32[128]{0:T(128)}, f32[128]{0:T(128)S(1)}, u32[]{:S(2)}) copy-start(f32[128]{0:T(128)S(1)} %get-tuple-element.72) | copy-start | bytes 1540
  463.7 5.4 copy-start.59
  463.7 6.6 copy-start.6
  470.2 31.1 %copy-start.42 = (f32[128,2]{0,1:T(2,128)}, f32[128,2]{0,1:T(2,128)S(1)}, u32[]{:S(2)}) copy-start(f32[128,2]{0,1:T(2,128)S(1)} %get-tuple-element.69) | copy-start | bytes 3076
  470.2 31.1 %copy-start.49 = (f32[128]{0:T(128)}, f32[128]{0:T(128)S(1)}, u32[]{:S(2)}) copy-start(f32[128]{0:T(128)S(1)} %get-tuple-element.100) | copy-start | bytes 1540
  470.2 31.1 %copy-start.51 = (f32[128]{0:T(128)}, f32[128]{0:T(128)S(1)}, u32[]{:S(2)}) copy-start(f32[128]{0:T(128)S(1)} %get-tuple-element.101) | copy-start | bytes 1540
  501.3 158.6 %reduce-scatter.11.cloned.1.call-start = ((), (), s32[]{:S(2)}) async-start(), calls=%async_computation.19 | async-start | bytes 9437184 | tf_op jit(solution)/shard_map/reduce_scatter | solution.py:128
  568.5 2.4 copy-start.63
  588.6 76.7 %copy-start.43 = (f32[128,2]{0,1:T(2,128)S(1)}, f32[128,2]{0,1:T(2,128)}, u32[]{:S(2)}) copy-start(f32[128,2]{0,1:T(2,128)} %copy-done.42) | copy-start | bytes 3076
  588.6 76.7 %copy-start.54 = (f32[128]{0:T(128)S(1)}, f32[128]{0:T(128)}, u32[]{:S(2)}) copy-start(f32[128]{0:T(128)} %copy-done.53) | copy-start | bytes 1540
  588.6 76.7 %copy-start.56 = (f32[128]{0:T(128)S(1)}, f32[128]{0:T(128)}, u32[]{:S(2)}) copy-start(f32[128]{0:T(128)} %copy-done.55) | copy-start | bytes 1540
  588.6 76.7 %copy-start.58 = (f32[128]{0:T(128)S(1)}, f32[128]{0:T(128)}, u32[]{:S(2)}) copy-start(f32[128]{0:T(128)} %get-tuple-element.68) | copy-start | bytes 1540
  588.6 99.3 %copy-start.8 = (bf16[128,2048]{1,0:T(8,128)(2,1)S(1)}, bf16[128,2048]{1,0:T(8,128)(2,1)}, u32[]{:S(2)}) copy-start(bf16[128,2048]{1,0:T(8,128)(2,1)} %reduce-scatter.7.cloned.1.call-done) | copy-start | bytes 1572868
  588.6 99.3 %copy-start.30 = (bf16[2048,6]{0,1:T(8,128)(2,1)S(1)}, bf16[2048,6]{0,1:T(8,128)(2,1)}, u32[]{:S(2)}) copy-start(bf16[2048,6]{0,1:T(8,128)(2,1)} %copy-done.29) | copy-start | bytes 73732
  588.7 99.3 %copy-start.32 = (f32[2048,1]{0,1:T(1,128)S(1)}, f32[2048,1]{0,1:T(1,128)}, u32[]{:S(2)}) copy-start(f32[2048,1]{0,1:T(1,128)} %copy-done.31) | copy-start | bytes 24580
  588.7 99.3 %copy-start.47 = (f32[128]{0:T(128)S(1)}, f32[128]{0:T(128)}, u32[]{:S(2)}) copy-start(f32[128]{0:T(128)} %copy-done.46) | copy-start | bytes 1540
  588.7 100.3 %copy-start.7 = (bf16[128,2048]{1,0:T(8,128)(2,1)S(1)}, bf16[128,2048]{1,0:T(8,128)(2,1)}, u32[]{:S(2)}) copy-start(bf16[128,2048]{1,0:T(8,128)(2,1)} %param.23) | copy-start | bytes 1572868
  588.7 100.3 %copy-start.41 = (f32[128]{0:T(128)S(1)}, f32[128]{0:T(128)}, u32[]{:S(2)}) copy-start(f32[128]{0:T(128)} %get-tuple-element.70) | copy-start | bytes 1540
  660.0 27.6 %all-to-all-start.4 = ((bf16[4,64,2048]{2,1,0:T(8,128)(2,1)}), bf16[4,64,2048]{2,1,0:T(8,128)(2,1)S(1)}, u32[]{:S(2)}, u32[]{:S(2)}) async-start(bf16[4,64,2048]{2,1,0:T(8,128)(2,1)} %bitcast.139), calls=%async_computation.7 | async-start | bytes 2097152 | tf_op jit(solution)/shard_map/all_to_all | solution.py:81
  665.1 70.6 %all-gather.17.cloned.1.call-start = ((), (), s32[]{:S(2)}) async-start(), calls=%async_computation.20 | async-start | bytes 2621440 | tf_op jit(solution)/shard_map/all_gather | solution.py:277
  687.5 2.8 copy-start.34
  687.6 2.8 copy-start.38
  687.6 48.1 %copy-start.61 = (bf16[4,128,512]{2,1,0:T(8,128)(2,1)S(1)}, bf16[4,128,512]{2,1,0:T(8,128)(2,1)}, u32[]{:S(2)}) copy-start(bf16[4,128,512]{2,1,0:T(8,128)(2,1)} %fusion.21) | copy-start | bytes 1572868
  689.0 50.9 %copy-start.10 = (f32[128,2048]{1,0:T(8,128)}, f32[128,2048]{1,0:T(8,128)S(1)}, u32[]{:S(2)}) copy-start(f32[128,2048]{1,0:T(8,128)S(1)} %get-tuple-element.107) | copy-start | bytes 3145732
  690.2 269.1 %reduce-scatter.17.cloned.1.call-start = ((), (), s32[]{:S(2)}) async-start(), calls=%async_computation.23 | async-start | bytes 2359296 | tf_op jit(solution)/shard_map/reduce_scatter | solution.py:280
  739.9 221.2 %reduce-scatter.13.cloned.1.call-start = ((), (), s32[]{:S(2)}) async-start(), calls=%async_computation.21 | async-start | bytes 2621440 | tf_op jit(solution)/shard_map/reduce_scatter | solution.py:305
  740.0 3.7 copy-start.3
  745.5 3.8 copy-start.4
  750.6 2.3 copy-start.23
  750.6 2.3 copy-start.24
  756.6 9.8 %copy-start.11 = (bf16[512,2048]{1,0:T(8,128)(2,1)S(1)}, bf16[512,2048]{1,0:T(8,128)(2,1)}, u32[]{:S(2)}) copy-start(bf16[512,2048]{1,0:T(8,128)(2,1)} %all-gather.7.cloned.1.call-done) | copy-start | bytes 6291460
  756.6 9.8 %copy-start.28 = (bf16[1,512,512]{2,1,0:T(8,128)(2,1)S(1)}, bf16[1,512,512]{2,1,0:T(8,128)(2,1)}, u32[]{:S(2)}) copy-start(bf16[1,512,512]{2,1,0:T(8,128)(2,1)} %copy.240) | copy-start | bytes 1572868
  756.6 9.8 %copy-start.36 = (f32[2048,1]{0,1:T(1,128)S(1)}, f32[2048,1]{0,1:T(1,128)}, u32[]{:S(2)}) copy-start(f32[2048,1]{0,1:T(1,128)} %copy-done.35) | copy-start | bytes 24580
  756.7 9.8 %copy-start.45 = (f32[512]{0:T(512)S(1)}, f32[512]{0:T(512)}, u32[]{:S(2)}) copy-start(f32[512]{0:T(512)} %copy-done.44) | copy-start | bytes 6148
  766.2 200.8 %reduce-scatter.15.cloned.1.call-start = ((), (), s32[]{:S(2)}) async-start(), calls=%async_computation.22 | async-start | bytes 7077888 | tf_op jit(solution)/shard_map/reduce_scatter | solution.py:309
  800.8 5.6 copy-start.13
  800.8 84.2 %all-to-all-start.5 = ((bf16[8,256,1408]{1,2,0:T(8,128)(2,1)}), bf16[8,256,1408]{1,2,0:T(8,128)(2,1)}, u32[]{:S(2)}, u32[]{:S(2)}) async-start(bf16[8,256,1408]{1,2,0:T(8,128)(2,1)} %copy.243), calls=%async_computation.11 | async-start | bytes 11534336 | tf_op jit(solution)/shard_map/all_to_all | solution.py:99
  915.4 47.1 %copy-start.50 = (f32[128]{0:T(128)S(1)}, f32[128]{0:T(128)}, u32[]{:S(2)}) copy-start(f32[128]{0:T(128)} %copy-done.49) | copy-start | bytes 1540
  915.4 47.1 %copy-start.52 = (f32[128]{0:T(128)S(1)}, f32[128]{0:T(128)}, u32[]{:S(2)}) copy-start(f32[128]{0:T(128)} %copy-done.51) | copy-start | bytes 1540
  962.5 7.0 copy-start.1
  (15 other events, 22.7 us)
Sparse Core Ops, SparseCore 0:
  9.6 45.4 all-gather.6
  57.5 46.9 all-gather.8
  106.5 28.1 all-gather.10
  139.2 41.5 reduce-scatter.6
  214.8 108.8 all-gather.12
  364.9 71.1 reduce-scatter.8
  501.4 53.8 all-gather.14
  588.8 71.1 reduce-scatter.10
  690.4 45.2 all-gather.16
  740.0 41.4 reduce-scatter.16
  783.9 41.6 reduce-scatter.12
  829.2 76.9 reduce-scatter.14
